TPU v7x, 32 devices: a whole 2x2x4 slice. The times are simulated.
32 devices in a mesh: spatial: 8 (over z, x), filter: 4 (over y, core).
Axes of the slice: x: 2, y: 2, z: 4, core: 2. Of those that a mesh axis runs over, the one named last changes fastest.
Arguments:
- volume_in: bfloat16 [128, 32, 8192], P('filter', 'spatial'), may hold values from -6 to 6
- filters_a: bfloat16 [27, 256, 128], P(None, 'filter'), may hold values from -0.109375 to 0.109375
- bias_a: bfloat16 [256], P('filter'), may hold values from -0.5 to 0.5
- filters_b: bfloat16 [27, 256, 256], P(None, 'filter'), may hold values from -0.078125 to 0.078125
- bias_b: bfloat16 [256], P('filter'), may hold values from -0.5 to 0.5
Outputs:
- volume_out: bfloat16 [256, 8, 512], P('filter', 'spatial')
All inputs are finite; a program needn't handle non-finite values.
Results may differ from a plain program's by a relative error of at most 0.0048.
Values may be sent and summed in bfloat16 or wider, within the bound.
A program may use at most 128 MiB of HBM per device.

v0:
```python
import jax
import jax.numpy as jnp
from jax import lax
from jax.sharding import PartitionSpec as P

ROWS = 64
COLS = 128


def shifted(block, axis, distance):
    devices = range(lax.axis_size(axis))
    route = [(i - distance, i) for i in devices if i - distance in devices]
    return lax.ppermute(block, axis, route)


def local_conv(block, weight, pad_rows, row_count, col_count):
    channels = block.shape[0]
    slices = block.shape[1]
    volume = block.reshape(1, channels, slices, row_count, col_count)
    kernel = weight.reshape(3, 3, 3, weight.shape[1], weight.shape[2])
    return lax.conv_general_dilated(
        volume,
        kernel,
        (2, 2, 2),
        ((0, 0), (pad_rows, pad_rows), (1, 1)),
        dimension_numbers=("NCDHW", "DHWOI", "NCDHW"),
        preferred_element_type=jnp.float32,
    )[0]


def activate(summed, bias_vec):
    summed = summed + bias_vec.astype(jnp.float32)[:, None, None, None]
    return jnp.where(summed > 0, summed, 0.2 * summed).astype(jnp.bfloat16)


def per_device(volume_in, filters_a, bias_a, filters_b, bias_b):
    slices = volume_in.shape[1]
    outputs = filters_a.shape[1]
    beneath = shifted(volume_in[:, -1:], "spatial", 1)
    extended = jnp.concatenate([beneath, volume_in], 1)
    zeros_first = jnp.zeros((outputs, slices // 2, ROWS // 2, COLS // 2), jnp.float32)
    weight_part = filters_a
    summed = zeros_first + local_conv(
        lax.all_gather(extended, "filter", axis=0, tiled=True), weight_part, 1, ROWS, COLS
    )
    hidden = activate(summed, bias_a).reshape(outputs, slices // 2, ROWS // 2 * (COLS // 2))
    beneath_two = shifted(hidden[:, -1:], "spatial", 1)
    extended_two = jnp.concatenate([beneath_two, hidden], 1)
    zeros_second = jnp.zeros((filters_b.shape[1], slices // 4, ROWS // 4, COLS // 4), jnp.float32)
    weight_part = filters_b
    summed_two = zeros_second + local_conv(
        lax.all_gather(extended_two, "filter", axis=0, tiled=True),
        weight_part,
        1,
        ROWS // 2,
        COLS // 2,
    )
    return activate(summed_two, bias_b).reshape(
        filters_b.shape[1], slices // 4, ROWS // 4 * (COLS // 4)
    )


def solution(mesh):
    in_specs = (
        P("filter", "spatial", None),
        P(None, "filter", None),
        P("filter"),
        P(None, "filter", None),
        P("filter"),
    )
    out_specs = P("filter", "spatial", None)
    return jax.shard_map(
        per_device, mesh=mesh, in_specs=in_specs, out_specs=out_specs, check_vma=False
    )
```

profile of v0, /device:TPU:0, one launch (start us, length us, event | category | flops | bytes accessed | tf_op | source)
XLA Modules:
  0.0 223.8 jit_solution(5031182525449573084)
XLA Ops:
  6.5 0.0 copy-start
  6.5 0.0 all-gather.3.cloned.1.call-start
  6.5 2.8 %copy.46 = bf16[32,4,8192]{2,0,1:T(8,128)(2,1)S(1)} copy(bf16[32,4,8192]{2,1,0:T(4,128)(2,1)} %param.5) | data formatting | bytes 4194304 | tf_op args[0]
  9.4 0.0 copy-start.2
  9.4 4.9 %collective-permute-start = (bf16[32,1,8192]{2,0,1:T(8,128)(2,1)S(1)}, bf16[32,1,8192]{2,0,1:T(8,128)(2,1)S(1)}, u32[]{:S(2)}, u32[]{:S(2)}) collective-permute-start(bf16[32,1,8192]{2,0,1:T(8,128)(2,1)S(1)} %slice.12), channel_id=1, source_target_pairs={{0,4},{4,8},{8,12},{12,16},{16,20},{20,24},{24,28},{1,5},{5,9},{9,... | collective-permute-start | bytes 1572872 | tf_op jit(solution)/shard_map/ppermute | solution.py:13
  14.3 11.1 %collective-permute-done = bf16[32,1,8192]{2,0,1:T(8,128)(2,1)S(1)} collective-permute-done((bf16[32,1,8192]{2,0,1:T(8,128)(2,1)S(1)}, bf16[32,1,8192]{2,0,1:T(8,128)(2,1)S(1)}, u32[]{:S(2)}, u32[]{:S(2)}) %collective-permute-start) | collective-permute-done | bytes 524320 | tf_op jit(solution)/shard_map/ppermute | solution.py:13
  25.4 1.8 pad_maximum_fusion
  27.2 0.0 all-gather.3.cloned.1.call-update
  27.2 0.0 all-gather.5.cloned.1.call-start
  27.3 0.0 copy-done.2
  27.3 72.5 %all-gather.3.cloned.1.call-done = bf16[128,5,8192]{2,0,1:T(8,128)(2,1)} async-done(((bf16[32,5,8192]{2,0,1:T(8,128)(2,1)}), bf16[128,5,8192]{2,0,1:T(8,128)(2,1)}) %all-gather.3.cloned.1.call-update) | async-done | bytes 10485776 | tf_op jit(solution)/shard_map/all_gather | solution.py:44
  99.8 14.2 %copy.48 = bf16[128,5,8192]{0,2,1:T(8,128)(2,1)} copy(bf16[128,5,8192]{2,0,1:T(8,128)(2,1)} %all-gather.3.cloned.1.call-done) | data formatting | bytes 20971520 | tf_op jit(solution)/shard_map/all_gather | solution.py:44
  114.0 14.7 %copy.61 = bf16[128,5,64,1,128]{0,2,4,1,3:T(8,128)(2,1)} copy(bf16[128,5,64,1,128]{0,4,2,1,3:T(8,128)(2,1)} %bitcast.31) | data formatting | bytes 20971520
  128.8 6.4 %pad.clone = bf16[128,5,64,1,144]{0,2,4,1,3:T(8,128)(2,1)S(1)} pad(bf16[128,5,64,1,128]{0,2,4,1,3:T(8,128)(2,1)} %copy.61, bf16[]{:T(256)} %constant.1), padding=0_0x0_0x0_0x0_0x1_15 | pad | bytes 22282242 | tf_op jit(solution)/shard_map/reshape | solution.py:19
  135.2 0.0 copy-start.1
  135.2 0.0 copy-start.4
  135.2 8.6 %copy.51 = bf16[128,5,64,1,8,18]{0,4,5,2,1,3:T(8,128)(2,1)S(1)} copy(bf16[128,5,64,1,8,18]{0,2,5,4,1,3:T(8,128)(2,1)S(1)} %bitcast.30) | data formatting | bytes 23592960 | tf_op jit(solution)/shard_map/conv_general_dilated | solution.py:21
  143.9 0.3 slice.13
  144.2 0.0 copy-done.1
  144.2 0.0 copy-done.4
  144.2 10.2 %fusion.12 = f32[2,32,8,9,64]{4,2,3,1,0:T(8,128)} fusion(bf16[3,3,3,64,128]{4,3,2,1,0:T(8,128)(2,1)S(1)} %bitcast.37, bf16[128,5,64,1,7,2]{0,4,5,2,1,3:T(8,128)(2,1)S(1)} %slice.13, bf16[128,5,64,1,8,18]{0,4,5,2,1,3:T(8,128)(2,1)S(1)} %copy.51, pred[8,9]{0,1:T(8,128)(4,1)S(1)} %copy-done.4), kind=kOutput, calls=%fused_computation.15 | convolution fusion | flops 2056814592 | bytes 14565448 | tf_op jit(solution)/shard_map/conv_general_dilated | solution.py:21
  154.5 2.1 copy.52
  156.6 0.2 slice_bitcast_fusion
  156.8 3.1 %copy.53 = f32[1,64,2,32,64]{4,3,1,2,0:T(8,128)} copy(f32[1,64,2,32,64]{1,3,4,2,0:T(8,128)S(1)} %slice_bitcast_fusion) | data formatting | bytes 2097152 | tf_op jit(solution)/shard_map/conv_general_dilated | solution.py:21
  159.8 0.0 copy-start.3
  159.8 2.1 squeeze.6
  161.9 0.2 fusion.18
  162.2 3.4 %collective-permute-start.1 = (bf16[64,1,2048]{2,0,1:T(8,128)(2,1)S(1)}, bf16[64,1,2048]{2,0,1:T(8,128)(2,1)S(1)}, u32[]{:S(2)}, u32[]{:S(2)}) collective-permute-start(bf16[64,1,2048]{2,0,1:T(8,128)(2,1)S(1)} %slice.15), channel_id=1, source_target_pairs={{0,4},{4,8},{8,12},{12,16},{16,20},{20,24},{24,28},{1,5},{5,9},{9,... | collective-permute-start | bytes 786440 | tf_op jit(solution)/shard_map/ppermute | solution.py:13
  165.6 6.0 %collective-permute-done.1 = bf16[64,1,2048]{2,0,1:T(8,128)(2,1)S(1)} collective-permute-done((bf16[64,1,2048]{2,0,1:T(8,128)(2,1)S(1)}, bf16[64,1,2048]{2,0,1:T(8,128)(2,1)S(1)}, u32[]{:S(2)}, u32[]{:S(2)}) %collective-permute-start.1) | collective-permute-done | bytes 262176 | tf_op jit(solution)/shard_map/ppermute | solution.py:13
  171.5 1.0 pad_maximum_fusion.1
  172.5 0.0 all-gather.5.cloned.1.call-update
  172.5 0.0 copy-done.3
  172.6 29.7 %all-gather.5.cloned.1.call-done = bf16[256,3,2048]{2,0,1:T(8,128)(2,1)} async-done(((bf16[64,3,2048]{2,0,1:T(8,128)(2,1)}), bf16[256,3,2048]{2,0,1:T(8,128)(2,1)}) %all-gather.5.cloned.1.call-update) | async-done | bytes 3145744 | tf_op jit(solution)/shard_map/all_gather | solution.py:52
  202.2 4.6 %copy.54 = bf16[256,3,2048]{0,2,1:T(8,128)(2,1)} copy(bf16[256,3,2048]{2,0,1:T(8,128)(2,1)} %all-gather.5.cloned.1.call-done) | data formatting | bytes 6291456 | tf_op jit(solution)/shard_map/all_gather | solution.py:52
  206.9 3.7 %copy.62 = bf16[256,3,32,1,64]{0,2,4,1,3:T(8,128)(2,1)S(1)} copy(bf16[256,3,32,1,64]{0,4,2,1,3:T(8,128)(2,1)} %bitcast.33) | data formatting | bytes 6291456
  210.6 0.4 pad.2.clone
  211.0 0.0 copy-start.5
  211.0 2.3 %copy.57 = bf16[256,3,32,1,8,10]{0,4,5,2,1,3:T(8,128)(2,1)S(1)} copy(bf16[256,3,32,1,8,10]{0,2,5,4,1,3:T(8,128)(2,1)S(1)} %bitcast.32) | data formatting | bytes 7864320 | tf_op jit(solution)/shard_map/conv_general_dilated | solution.py:21
  213.3 0.2 slice.16
  213.5 0.0 copy-done
  213.5 0.0 copy-done.5
  213.5 2.5 %fusion.15 = f32[1,16,8,5,64]{4,2,3,1,0:T(8,128)S(1)} fusion(bf16[3,3,3,64,256]{4,3,2,1,0:T(8,128)(2,1)S(1)} %bitcast.29, bf16[256,3,32,1,7,2]{0,4,5,2,1,3:T(8,128)(2,1)S(1)} %slice.16, bf16[256,3,32,1,8,10]{0,4,5,2,1,3:T(8,128)(2,1)S(1)} %copy.57, pred[8,5]{0,1:T(8,128)(4,1)S(1)} %copy-done.5), kind=kOutput, calls=%fused_computation.16 | convolution fusion | flops 568631296 | bytes 5668904 | tf_op jit(solution)/shard_map/conv_general_dilated | solution.py:21
  216.0 0.1 copy.58
  216.1 0.1 copy.59
  216.1 0.1 copy.60
  216.3 0.7 fusion.19
  (5 shorter events, 0.1 us)
Async XLA Ops:
  6.5 206.9 %copy-start = (bf16[27,64,256]{2,1,0:T(8,128)(2,1)S(1)}, bf16[27,64,256]{2,1,0:T(8,128)(2,1)}, u32[]{:S(2)}) copy-start(bf16[27,64,256]{2,1,0:T(8,128)(2,1)} %param.8) | copy-start | bytes 2654212
  6.5 93.3 %all-gather.3.cloned.1.call-start = ((), (), s32[]{:S(2)}) async-start(), calls=%async_computation | async-start | bytes 13107200 | tf_op jit(solution)/shard_map/all_gather | solution.py:44
  9.4 17.9 %copy-start.2 = (bf16[64]{0:T(256)(128)(2,1)S(1)}, bf16[64]{0:T(256)(128)(2,1)}, u32[]{:S(2)}) copy-start(bf16[64]{0:T(256)(128)(2,1)} %param.7) | copy-start | bytes 388
  9.4 16.0 %collective-permute-start = (bf16[32,1,8192]{2,0,1:T(8,128)(2,1)S(1)}, bf16[32,1,8192]{2,0,1:T(8,128)(2,1)S(1)}, u32[]{:S(2)}, u32[]{:S(2)}) collective-permute-start(bf16[32,1,8192]{2,0,1:T(8,128)(2,1)S(1)} %slice.12), channel_id=1, source_target_pairs={{0,4},{4,8},{8,12},{12,16},{16,20},{20,24},{24,28},{1,5},{5,9},{9,... | collective-permute-start | bytes 1572872 | tf_op jit(solution)/shard_map/ppermute | solution.py:13
  27.2 175.0 %all-gather.5.cloned.1.call-start = ((), (), s32[]{:S(2)}) async-start(), calls=%async_computation.1 | async-start | bytes 3932160 | tf_op jit(solution)/shard_map/all_gather | solution.py:52
  135.2 9.0 %copy-start.1 = (bf16[27,64,128]{2,1,0:T(8,128)(2,1)S(1)}, bf16[27,64,128]{2,1,0:T(8,128)(2,1)}, u32[]{:S(2)}) copy-start(bf16[27,64,128]{2,1,0:T(8,128)(2,1)} %param.6) | copy-start | bytes 1327108
  135.2 9.0 %copy-start.4 = (pred[8,9]{0,1:T(8,128)(4,1)S(1)}, pred[8,9]{0,1:T(8,128)(4,1)}, u32[]{:S(2)}) copy-start(pred[8,9]{0,1:T(8,128)(4,1)} %constant.16) | copy-start | bytes 220
  159.8 12.7 %copy-start.3 = (bf16[64]{0:T(256)(128)(2,1)S(1)}, bf16[64]{0:T(256)(128)(2,1)}, u32[]{:S(2)}) copy-start(bf16[64]{0:T(256)(128)(2,1)} %param.9) | copy-start | bytes 388
  162.2 9.4 %collective-permute-start.1 = (bf16[64,1,2048]{2,0,1:T(8,128)(2,1)S(1)}, bf16[64,1,2048]{2,0,1:T(8,128)(2,1)S(1)}, u32[]{:S(2)}, u32[]{:S(2)}) collective-permute-start(bf16[64,1,2048]{2,0,1:T(8,128)(2,1)S(1)} %slice.15), channel_id=1, source_target_pairs={{0,4},{4,8},{8,12},{12,16},{16,20},{20,24},{24,28},{1,5},{5,9},{9,... | collective-permute-start | bytes 786440 | tf_op jit(solution)/shard_map/ppermute | solution.py:13
  211.0 2.5 %copy-start.5 = (pred[8,5]{0,1:T(8,128)(4,1)S(1)}, pred[8,5]{0,1:T(8,128)(4,1)}, u32[]{:S(2)}) copy-start(pred[8,5]{0,1:T(8,128)(4,1)} %constant.15) | copy-start | bytes 124
Sparse Core Ops, SparseCore 0:
  27.4 72.4 all-gather.2
  172.7 29.5 all-gather.4
where the time goes:
time: 225 us; the launch traced here: 224 us
  waiting for transfers between devices  119 us (53%)
  local copies, waits for them, and re-layouts  66.2 us (29%)
  between operations  13.6 us (6%)
  matrix products  12.7 us (6%)
  starting transfers between devices  8.31 us (4%)
  other arithmetic  3.7 us (2%)
    all_gather x1, waiting for transfers between devices, per_device(): lax.all_gather(extended, 'filter', axis=0, tiled=True)  72.5 us
    all_gather x1, waiting for transfers between devices, per_device(): lax.all_gather(extended_two, 'filter', axis=0, tiled=True)  29.7 us
    unnamed x15, local copies, waits for them, and re-layouts  21.3 us
    ppermute x2, waiting for transfers between devices, shifted(): return lax.ppermute(block, axis, route)  17.1 us
    conv_general_dilated x10, local copies, waits for them, and re-layouts, local_conv(): lax.conv_general_dilated(volume, kernel, (2, 2, 2), ((0, 0), (pad_rows, p...  17 us
    all_gather x1, local copies, waits for them, and re-layouts, per_device(): lax.all_gather(extended, 'filter', axis=0, tiled=True)  14.2 us
    conv_general_dilated x2, matrix products, local_conv(): lax.conv_general_dilated(volume, kernel, (2, 2, 2), ((0, 0), (pad_rows, p...  12.7 us
    ppermute x2, starting transfers between devices, shifted(): return lax.ppermute(block, axis, route)  8.26 us
  transfers between devices with their start and end apart: 4, of which 4 were waited for; matrix products, arithmetic and copies ran while one was open for 0% of the time, Pallas kernels for 0%

commit v1 on v0

--- a/solution.py
+++ b/solution.py
@@ -5,6 +5,27 @@
 
 ROWS = 64
 COLS = 128
+
+
+def ring_gather(x, axis, dim):
+    peers, index, rows = (lax.axis_size(axis), lax.axis_index(axis), x.shape[dim])
+    forward = [(i, (i + 1) % peers) for i in range(peers)]
+    backward = [(i, (i - 1) % peers) for i in range(peers)]
+    out = jnp.zeros((*x.shape[:dim], peers * rows, *x.shape[dim + 1 :]), x.dtype)
+    out = lax.dynamic_update_slice_in_dim(out, x, index * rows, axis=dim)
+    from_left = from_right = x
+    half = peers // 2
+    for step in range(1, half + 1):
+        from_left = lax.ppermute(from_left, axis, forward)
+        out = lax.dynamic_update_slice_in_dim(
+            out, from_left, (index - step) % peers * rows, axis=dim
+        )
+        if step < peers - half:
+            from_right = lax.ppermute(from_right, axis, backward)
+            out = lax.dynamic_update_slice_in_dim(
+                out, from_right, (index + step) % peers * rows, axis=dim
+            )
+    return out
 
 
 def shifted(block, axis, distance):
@@ -41,7 +62,7 @@
     zeros_first = jnp.zeros((outputs, slices // 2, ROWS // 2, COLS // 2), jnp.float32)
     weight_part = filters_a
     summed = zeros_first + local_conv(
-        lax.all_gather(extended, "filter", axis=0, tiled=True), weight_part, 1, ROWS, COLS
+        ring_gather(extended, "filter", 0), weight_part, 1, ROWS, COLS
     )
     hidden = activate(summed, bias_a).reshape(outputs, slices // 2, ROWS // 2 * (COLS // 2))
     beneath_two = shifted(hidden[:, -1:], "spatial", 1)

time: 225 us -> 691 us (3.07); the launches traced: 224 us -> 679 us
  local copies, waits for them, and re-layouts: 66.2 us -> 533 us
  waiting for transfers between devices: 119 us -> 96.7 us
  other arithmetic: 3.7 us -> 11.5 us
    dynamic_update_slice x0 -> x4, local copies, waits for them, and re-layouts: none -> 431 us  [the longest x2 224 us: ring_gather(): lax.dynamic_update_slice_in_dim(out, from_left, (index - step) % peers *...]
    all_gather x1 -> x0, waiting for transfers between devices: 72.5 us -> none  [per_device(): lax.all_gather(extended, 'filter', axis=0, tiled=True)]
    ppermute x0 -> x3, waiting for transfers between devices: none -> 55.8 us  [the longest x2 55.8 us: ring_gather(): from_left = lax.ppermute(from_left, axis, forward)]
    ppermute x0 -> x4, local copies, waits for them, and re-layouts: none -> 26.9 us  [the longest x2 16.5 us: ring_gather(): from_left = lax.ppermute(from_left, axis, forward)]
    all_gather x1 -> x0, local copies, waits for them, and re-layouts: 14.2 us -> none  [per_device(): lax.all_gather(extended, 'filter', axis=0, tiled=True)]
    concatenate x0 -> x1, local copies, waits for them, and re-layouts: none -> 9.76 us  [per_device(): extended = jnp.concatenate([beneath, volume_in], 1)]
    ppermute x2, waiting for transfers between devices: 17.1 us -> 8.36 us  [shifted(): return lax.ppermute(block, axis, route)]
    concatenate x1, other arithmetic: 1.78 us -> 9.61 us  [per_device(): extended = jnp.concatenate([beneath, volume_in], 1)]
  transfers between devices with their start and end apart: 4 -> 6, of which waited for: 4 -> 4; matrix products, arithmetic and copies ran while one was open for 0% -> 51% of each run, Pallas kernels for 0% -> 0%
where the time goes in v1:
time: 691 us; the launch traced here: 679 us
  local copies, waits for them, and re-layouts  533 us (77%)
  waiting for transfers between devices  96.7 us (14%)
  between operations  13.6 us (2%)
  matrix products  12.7 us (2%)
  other arithmetic  11.5 us (2%)
  starting transfers between devices  11.4 us (2%)
    dynamic_update_slice x2, local copies, waits for them, and re-layouts, ring_gather(): lax.dynamic_update_slice_in_dim(out, from_left, (index - step) % peers *...  224 us
    dynamic_update_slice x1, local copies, waits for them, and re-layouts, ring_gather(): lax.dynamic_update_slice_in_dim(out, from_right, (index + step) % peers *...  112 us
    dynamic_update_slice x1, local copies, waits for them, and re-layouts, ring_gather(): out = lax.dynamic_update_slice_in_dim(out, x, index * rows, axis=dim)  95 us
    ppermute x2, waiting for transfers between devices, ring_gather(): from_left = lax.ppermute(from_left, axis, forward)  55.8 us
    all_gather x1, waiting for transfers between devices, per_device(): lax.all_gather(extended_two, 'filter', axis=0, tiled=True)  32.5 us
    unnamed x16, local copies, waits for them, and re-layouts  27 us
    conv_general_dilated x10, local copies, waits for them, and re-layouts, local_conv(): lax.conv_general_dilated(volume, kernel, (2, 2, 2), ((0, 0), (pad_rows, p...  17 us
    ppermute x2, local copies, waits for them, and re-layouts, ring_gather(): from_left = lax.ppermute(from_left, axis, forward)  16.5 us
  transfers between devices with their start and end apart: 6, of which 4 were waited for; matrix products, arithmetic and copies ran while one was open for 51% of the time, Pallas kernels for 0%

profile of v1, /device:TPU:0, one launch (start us, length us, event | category | flops | bytes accessed | tf_op | source)
XLA Modules:
  0.0 679.0 jit_solution(14591057789075485718)
XLA Ops:
  6.5 2.9 slice.6
  9.5 0.6 copy.89
  10.1 4.9 collective-permute-start
  15.0 8.0 %copy.71 = bf16[32,4,8192]{0,2,1:T(8,128)(2,1)} copy(bf16[32,4,8192]{2,1,0:T(4,128)(2,1)} %param.5) | data formatting | bytes 4194304 | tf_op args[0]
  22.9 3.2 collective-permute-done
  26.1 1.0 copy.70
  27.1 9.6 %pad_maximum_fusion = bf16[32,5,8192]{0,2,1:T(8,128)(2,1)} fusion(bf16[32,4,8192]{0,2,1:T(8,128)(2,1)} %copy.71, bf16[32,1,8192]{0,2,1:T(8,128)(2,1)S(1)} %copy.70), kind=kLoop, calls=%fused_computation.5 | loop fusion | flops 1310720 | bytes 5242880 | tf_op jit(solution)/shard_map/concatenate | solution.py:61
  36.7 9.8 %copy.72 = bf16[32,5,8192]{2,0,1:T(8,128)(2,1)} copy(bf16[32,5,8192]{0,2,1:T(8,128)(2,1)} %pad_maximum_fusion) | data formatting | bytes 5242880 | tf_op jit(solution)/shard_map/concatenate | solution.py:61
  46.5 1.7 collective-permute-start.2
  48.3 55.7 %collective-permute-done.1 = bf16[32,5,8192]{2,0,1:T(8,128)(2,1)S(1)} collective-permute-done((bf16[32,5,8192]{2,0,1:T(8,128)(2,1)}, bf16[32,5,8192]{2,0,1:T(8,128)(2,1)S(1)}, u32[]{:S(2)}, u32[]{:S(2)}) %collective-permute-start.1) | collective-permute-done | bytes 2621472 | tf_op jit(solution)/shard_map/ppermute | solution.py:19
  104.0 0.4 collective-permute-start.3
  104.4 5.2 broadcast_in_dim.2
  109.5 95.0 %dynamic_update_slice.12 = bf16[128,5,8192]{0,2,1:T(8,128)(2,1)} dynamic-update-slice(bf16[128,5,8192]{0,2,1:T(8,128)(2,1)} %broadcast_in_dim.2, bf16[32,5,8192]{0,2,1:T(8,128)(2,1)} %pad_maximum_fusion, s32[]{:T(128)S(6)} %select_n.45, s32[]{:T(128)} %constant.36.clone.1, s32[]{:T(128)} %constant.36.clone.1) | dynamic-update-slice | bytes 5242884 | tf_op jit(solution)/shard_map/dynamic_update_slice | solution.py:15
  204.5 7.2 %copy.73 = bf16[32,5,8192]{0,2,1:T(8,128)(2,1)} copy(bf16[32,5,8192]{2,0,1:T(8,128)(2,1)S(1)} %collective-permute-done.1) | data formatting | bytes 5242880 | tf_op jit(solution)/shard_map/ppermute | solution.py:19
  211.7 111.9 %dynamic_update_slice.13 = bf16[128,5,8192]{0,2,1:T(8,128)(2,1)} dynamic-update-slice(bf16[128,5,8192]{0,2,1:T(8,128)(2,1)} %dynamic_update_slice.12, bf16[32,5,8192]{0,2,1:T(8,128)(2,1)} %copy.73, s32[]{:T(128)S(6)} %select_n.47, s32[]{:T(128)} %constant.36.clone.1, s32[]{:T(128)} %constant.36.clone.1) | dynamic-update-slice | bytes 5242884 | tf_op jit(solution)/shard_map/dynamic_update_slice | solution.py:20
  323.6 9.4 %copy.75 = bf16[32,5,8192]{0,2,1:T(8,128)(2,1)} copy(bf16[32,5,8192]{2,0,1:T(8,128)(2,1)} %collective-permute-done.2) | data formatting | bytes 5242880 | tf_op jit(solution)/shard_map/ppermute | solution.py:24
  332.9 111.9 %dynamic_update_slice.14 = bf16[128,5,8192]{0,2,1:T(8,128)(2,1)} dynamic-update-slice(bf16[128,5,8192]{0,2,1:T(8,128)(2,1)} %dynamic_update_slice.13, bf16[32,5,8192]{0,2,1:T(8,128)(2,1)} %copy.75, s32[]{:T(128)S(6)} %select_n.49, s32[]{:T(128)} %constant.36.clone.1, s32[]{:T(128)} %constant.36.clone.1) | dynamic-update-slice | bytes 5242884 | tf_op jit(solution)/shard_map/dynamic_update_slice | solution.py:25
  444.8 9.4 %copy.76 = bf16[32,5,8192]{0,2,1:T(8,128)(2,1)} copy(bf16[32,5,8192]{2,0,1:T(8,128)(2,1)} %collective-permute-done.3) | data formatting | bytes 5242880 | tf_op jit(solution)/shard_map/ppermute | solution.py:19
  454.2 111.9 %dynamic_update_slice.15 = bf16[128,5,8192]{0,2,1:T(8,128)(2,1)} dynamic-update-slice(bf16[128,5,8192]{0,2,1:T(8,128)(2,1)} %dynamic_update_slice.14, bf16[32,5,8192]{0,2,1:T(8,128)(2,1)} %copy.76, s32[]{:T(128)S(6)} %select_n.51, s32[]{:T(128)} %constant.36.clone.1, s32[]{:T(128)} %constant.36.clone.1) | dynamic-update-slice | bytes 5242884 | tf_op jit(solution)/shard_map/dynamic_update_slice | solution.py:20
  566.1 14.7 %copy.90 = bf16[128,5,64,1,128]{0,2,4,1,3:T(8,128)(2,1)} copy(bf16[128,5,64,1,128]{0,4,2,1,3:T(8,128)(2,1)} %bitcast.31) | data formatting | bytes 20971520
  580.8 6.4 pad.clone
  587.2 0.0 copy-start.1
  587.2 0.0 copy-start.4
  587.3 8.7 %copy.79 = bf16[128,5,64,1,8,18]{0,4,5,2,1,3:T(8,128)(2,1)S(1)} copy(bf16[128,5,64,1,8,18]{0,2,5,4,1,3:T(8,128)(2,1)S(1)} %bitcast.30) | data formatting | bytes 23592960 | tf_op jit(solution)/shard_map/conv_general_dilated | solution.py:42
  596.0 0.3 slice.12
  596.3 10.2 %fusion.12 = f32[2,32,8,9,64]{4,2,3,1,0:T(8,128)} fusion(bf16[3,3,3,64,128]{4,3,2,1,0:T(8,128)(2,1)S(1)} %bitcast.37, bf16[128,5,64,1,7,2]{0,4,5,2,1,3:T(8,128)(2,1)S(1)} %slice.12, bf16[128,5,64,1,8,18]{0,4,5,2,1,3:T(8,128)(2,1)S(1)} %copy.79, pred[8,9]{0,1:T(8,128)(4,1)S(1)} %copy-done.4), kind=kOutput, calls=%fused_computation.15 | convolution fusion | flops 2056814592 | bytes 14565448 | tf_op jit(solution)/shard_map/conv_general_dilated | solution.py:42
  606.5 2.1 copy.80
  608.7 0.0 copy-start.3
  608.7 0.2 slice_bitcast_fusion
  608.9 3.1 copy.81
  611.9 2.1 squeeze.6
  614.0 0.2 fusion.18
  614.3 4.4 collective-permute-start.4
  618.7 5.2 collective-permute-done.4
  623.9 1.0 pad_maximum_fusion.1
  624.9 0.0 all-gather.2.cloned.1.call-update
  624.9 32.5 %all-gather.2.cloned.1.call-done = bf16[256,3,2048]{2,0,1:T(8,128)(2,1)} async-done(((bf16[64,3,2048]{2,0,1:T(8,128)(2,1)}), bf16[256,3,2048]{2,0,1:T(8,128)(2,1)}) %all-gather.2.cloned.1.call-update) | async-done | bytes 3145744 | tf_op jit(solution)/shard_map/all_gather | solution.py:73
  657.4 4.6 copy.82
  662.1 3.7 copy.91
  665.7 0.0 copy-start.5
  665.8 0.4 pad.2.clone
  666.2 2.3 copy.85
  668.5 0.2 slice.15
  668.7 2.5 fusion.15
  671.1 0.1 copy.86
  671.2 0.1 copy.87
  671.3 0.1 copy.88
  671.5 0.7 fusion.19
  (16 shorter events, 0.1 us)
Async XLA Ops:
  6.5 662.1 %copy-start = (bf16[27,64,256]{2,1,0:T(8,128)(2,1)S(1)}, bf16[27,64,256]{2,1,0:T(8,128)(2,1)}, u32[]{:S(2)}) copy-start(bf16[27,64,256]{2,1,0:T(8,128)(2,1)} %param.8) | copy-start | bytes 2654212
  6.5 650.9 %all-gather.2.cloned.1.call-start = ((), (), s32[]{:S(2)}) async-start(), calls=%async_computation | async-start | bytes 3932160 | tf_op jit(solution)/shard_map/all_gather | solution.py:73
  10.1 16.0 %collective-permute-start = (bf16[32,1,8192]{2,0,1:T(8,128)(2,1)S(1)}, bf16[32,1,8192]{2,0,1:T(8,128)(2,1)S(1)}, u32[]{:S(2)}, u32[]{:S(2)}) collective-permute-start(bf16[32,1,8192]{2,0,1:T(8,128)(2,1)S(1)} %copy.89), channel_id=1, source_target_pairs={{0,4},{4,8},{8,12},{12,16},{16,20},{20,24},{24,28},{1,5},{5,9},{9,... | collective-permute-start | bytes 1572872 | tf_op jit(solution)/shard_map/ppermute | solution.py:34
  36.7 67.6 %copy-start.2 = (bf16[64]{0:T(256)(128)(2,1)S(1)}, bf16[64]{0:T(256)(128)(2,1)}, u32[]{:S(2)}) copy-start(bf16[64]{0:T(256)(128)(2,1)} %param.7) | copy-start | bytes 388
  46.5 57.5 %collective-permute-start.1 = (bf16[32,5,8192]{2,0,1:T(8,128)(2,1)}, bf16[32,5,8192]{2,0,1:T(8,128)(2,1)S(1)}, u32[]{:S(2)}, u32[]{:S(2)}) collective-permute-start(bf16[32,5,8192]{2,0,1:T(8,128)(2,1)} %copy.72), channel_id=1, source_target_pairs={{0,1},{1,2},{2,3},{3,0},{4,5},{5,6},{6,7},{7,4},{8,9},{9,10},{10,1... | collective-permute-start | bytes 7864328 | tf_op jit(solution)/shard_map/ppermute | solution.py:19
  46.5 277.1 %collective-permute-start.2 = (bf16[32,5,8192]{2,0,1:T(8,128)(2,1)}, bf16[32,5,8192]{2,0,1:T(8,128)(2,1)}, u32[]{:S(2)}, u32[]{:S(2)}) collective-permute-start(bf16[32,5,8192]{2,0,1:T(8,128)(2,1)} %copy.72), channel_id=1, source_target_pairs={{0,3},{1,0},{2,1},{3,2},{4,7},{5,4},{6,5},{7,6},{8,11},{9,8},{10,9... | collective-permute-start | bytes 7864328 | tf_op jit(solution)/shard_map/ppermute | solution.py:24
  104.0 340.8 %collective-permute-start.3 = (bf16[32,5,8192]{2,0,1:T(8,128)(2,1)S(1)}, bf16[32,5,8192]{2,0,1:T(8,128)(2,1)}, u32[]{:S(2)}, u32[]{:S(2)}) collective-permute-start(bf16[32,5,8192]{2,0,1:T(8,128)(2,1)S(1)} %collective-permute-done.1), channel_id=1, source_target_pairs={{0,1},{1,2},{2,3},{3,0},{4,5},{5,6},{6,7},{7,4},{8,9},{9,10},{10,1... | collective-permute-start | bytes 7864328 | tf_op jit(solution)/shard_map/ppermute | solution.py:19
  587.2 9.1 %copy-start.1 = (bf16[27,64,128]{2,1,0:T(8,128)(2,1)S(1)}, bf16[27,64,128]{2,1,0:T(8,128)(2,1)}, u32[]{:S(2)}) copy-start(bf16[27,64,128]{2,1,0:T(8,128)(2,1)} %param.6) | copy-start | bytes 1327108
  587.2 9.1 %copy-start.4 = (pred[8,9]{0,1:T(8,128)(4,1)S(1)}, pred[8,9]{0,1:T(8,128)(4,1)}, u32[]{:S(2)}) copy-start(pred[8,9]{0,1:T(8,128)(4,1)} %constant.55) | copy-start | bytes 220
  608.7 16.2 %copy-start.3 = (bf16[64]{0:T(256)(128)(2,1)S(1)}, bf16[64]{0:T(256)(128)(2,1)}, u32[]{:S(2)}) copy-start(bf16[64]{0:T(256)(128)(2,1)} %param.9) | copy-start | bytes 388
  614.3 9.6 %collective-permute-start.4 = (bf16[64,1,2048]{2,0,1:T(8,128)(2,1)S(1)}, bf16[64,1,2048]{2,0,1:T(8,128)(2,1)S(1)}, u32[]{:S(2)}, u32[]{:S(2)}) collective-permute-start(bf16[64,1,2048]{2,0,1:T(8,128)(2,1)S(1)} %slice.14), channel_id=1, source_target_pairs={{0,4},{4,8},{8,12},{12,16},{16,20},{20,24},{24,28},{1,5},{5,9},{9,... | collective-permute-start | bytes 786440 | tf_op jit(solution)/shard_map/ppermute | solution.py:34
  665.7 2.9 copy-start.5
Sparse Core Ops, SparseCore 0:
  625.0 32.3 all-gather.1
